TPU v7x, 256 devices: a whole 4x4x8 slice. The times are simulated.
256 devices in a mesh: blk: 16 (over z, x_hi), leaf: 8 (over y, core), rhs: 2 (over x_lo).
Axes of the slice: x: 4 (x_hi: 2, x_lo: 2; x = x_hi * 2 + x_lo), y: 4, z: 8, core: 2. Of those that a mesh axis runs over, the one named last changes fastest.
Arguments:
- residual: float32 [32, 8, 65536], P('rhs', 'leaf', 'blk'), may hold values from -160 to 160
- points: float32 [3, 8, 65536], P(None, 'leaf', 'blk'), may hold values from -12330 to 12330
- noise: float32 [8, 65536], P('leaf', 'blk'), may hold values from 1 to 2
- block_list: int32 [8, 8, 256], P('leaf'), may hold values from 0 to 1, as said below
Outputs:
- correction: float32 [32, 8, 65536], P('rhs', 'leaf', 'blk')
- new_residual: float32 [32, 8, 65536], P('rhs', 'leaf', 'blk')
- basis: float32 [128, 8, 65536], P('rhs', 'leaf', 'blk')
Inputs may be any that keep to these rules, and one draw needn't show every extreme that they name: The list is symmetric: block_list[t, k, i] == block_list[t, 7 - k, (i + d) mod 256] with d the offset of entry k.
All inputs are finite; a program needn't handle non-finite values.
Results may differ from a plain program's by a relative error of at most 0.007.
Values sent between devices are 32-bit elements; how exact they have to be, the bound alone decides.
A program may use at most 128 MiB of HBM per device.

v0:
```python
import jax
import jax.numpy as jnp
from jax import lax
from jax.sharding import PartitionSpec as P

M = 32
S = 4
BS = 256
REACH = 4
SUPPORT = 1408
centre_shift = 1.5
amplitude = 1.1
exact = lax.Precision.HIGHEST


def extended(x, sides, width):
    for axis, dim in sides:
        count, length = (lax.axis_size(axis), x.shape[dim])
        up = [(i, (i + 1) % count) for i in range(count)]
        down = [(j, i) for i, j in up]
        last = lax.slice_in_dim(x, length - width, length, axis=dim)
        leading = lax.slice_in_dim(x, 0, width, axis=dim)
        before = lax.ppermute(last, axis, up)
        after = lax.ppermute(leading, axis, down)
        x = jnp.concatenate([before, x, after], axis=dim)
    return x


def kernel_tile(near_points, own_points):
    squared = (near_points[0][:, None] - own_points[0][None, :]) ** 2
    squared = squared + (near_points[1][:, None] - own_points[1][None, :]) ** 2
    squared = squared + (near_points[2][:, None] - own_points[2][None, :]) ** 2
    radius = jnp.sqrt(squared) / SUPPORT
    remain = jnp.maximum(1.0 - radius, 0.0)
    return remain * remain * (remain * remain) * (4.0 * radius + 1.0) * (amplitude / SUPPORT)


def band_product(field_wide, points_wide, weights, rows_out):
    per_turn = rows_out // 8
    count = field_wide.shape[0]

    def turn(carry, index):
        pieces = []
        for inner in range(per_turn):
            block = index * per_turn + inner
            own_points = lax.dynamic_slice_in_dim(points_wide, (block + REACH) * BS, BS, 1)
            total = jnp.zeros((count, BS), jnp.float32)
            for offset in range(2 * REACH + 1):
                column_at = (block + offset) * BS
                near_points = lax.dynamic_slice_in_dim(points_wide, column_at, BS, 1)
                near_field = lax.dynamic_slice_in_dim(field_wide, column_at, BS, 1)
                listed = lax.dynamic_index_in_dim(weights[offset], block, 0, False)
                tile = kernel_tile(near_points, own_points) * listed
                total = total + jnp.dot(near_field, tile, precision=exact)
            pieces.append(total)
        return (carry, jnp.concatenate(pieces, axis=1))

    carry, parts = lax.scan(turn, jnp.zeros((), jnp.int32), jnp.arange(8, dtype=jnp.int32))
    return jnp.moveaxis(parts, 0, 1).reshape(count, rows_out * BS)


def galerkin(gram, count_points, count_sides):
    normed = gram / count_points
    basis_count = normed.shape[0] - count_sides
    gram_basis = normed[:basis_count, :basis_count]
    factor_low = jnp.linalg.cholesky(gram_basis)
    inverse_low = lax.linalg.triangular_solve(
        factor_low, jnp.eye(basis_count, dtype=jnp.float32), left_side=True, lower=True
    )
    cross = normed[:basis_count, count_sides:] + centre_shift * gram_basis
    projected = jnp.dot(
        jnp.dot(inverse_low, cross, precision=exact), inverse_low.T, precision=exact
    )
    projected = 0.5 * (projected + projected.T)
    small_side = jnp.dot(inverse_low, gram_basis[:, :count_sides], precision=exact)
    proj_factor = jnp.linalg.cholesky(projected)
    halfway = lax.linalg.triangular_solve(proj_factor, small_side, left_side=True, lower=True)
    coeffs = lax.linalg.triangular_solve(
        proj_factor, halfway, left_side=True, lower=True, transpose_a=True
    )
    combo = jnp.dot(coeffs.T, inverse_low, precision=exact)
    return (inverse_low, combo)


def row_products(rows):
    return lax.dot_general(rows, rows, (((1,), (1,)), ((), ())), precision=exact)


def local(residual, points, noise, block_list):
    field = residual[:, 0]
    coords = points[:, 0]
    nugget = noise[0]
    own_rows = field.shape[1]
    own_blocks = own_rows // BS
    first_block = lax.axis_index("blk") * own_blocks
    listed = block_list[0].astype(jnp.float32)
    nine = jnp.concatenate(
        [listed[:REACH], jnp.ones((1, listed.shape[1]), jnp.float32), listed[REACH:]], axis=0
    )
    margin = S * REACH
    wrapped = jnp.concatenate([nine[:, -margin:], nine, nine[:, :margin]], axis=1)
    powers = [field]
    rim = REACH * BS
    coords_wide = extended(coords, (("blk", 1),), rim)
    own_weights = lax.dynamic_slice_in_dim(wrapped, first_block + margin, own_blocks, 1)
    current = field
    for power_step in range(S):
        widened = extended(current, (("blk", 1),), rim)
        current = (
            band_product(widened, coords_wide, own_weights, own_blocks)
            + (nugget - centre_shift) * current
        )
        powers.append(current)
    half_panel = jnp.stack(powers, axis=0)
    count_points = own_rows * lax.axis_size("blk") * lax.axis_size("leaf")
    sides_here = field.shape[0]
    whole = lax.all_gather(half_panel, "rhs", axis=1, tiled=True)
    flat = whole.reshape(-1, own_rows)
    gram = lax.psum(row_products(flat), ("blk", "leaf"))
    inverse_low, combo = galerkin(gram, count_points, M)
    first_rows = flat[: S * M]
    image = flat[M:] + centre_shift * first_rows
    part = lax.axis_index("rhs")
    basis_here = S * M // lax.axis_size("rhs")
    mine_low = lax.dynamic_slice_in_dim(inverse_low, part * basis_here, basis_here, 0)
    mine_combo = lax.dynamic_slice_in_dim(combo, part * sides_here, sides_here, 0)
    correction = jnp.dot(mine_combo, first_rows, precision=exact)
    new_residual = field - jnp.dot(mine_combo, image, precision=exact)
    basis = jnp.dot(mine_low, first_rows, precision=exact)
    return (correction[:, None], new_residual[:, None], basis[:, None])


def solution(mesh):
    placed = (
        P("rhs", "leaf", "blk"),
        P(None, "leaf", "blk"),
        P("leaf", "blk"),
        P("leaf", None, None),
    )
    return jax.shard_map(
        local,
        mesh=mesh,
        in_specs=placed,
        out_specs=(P("rhs", "leaf", "blk"), P("rhs", "leaf", "blk"), P("rhs", "leaf", "blk")),
        check_vma=False,
    )
```

profile of v0, /device:TPU:2, one launch (start us, length us, event | category | flops | bytes accessed | tf_op | source)
XLA Modules:
  0.0 2114.2 jit_solution(17787421845742051918)
XLA Ops:
  7.2 0.8 copy.48
  8.1 2.2 collective-permute-start.2
  10.3 5.4 collective-permute-start.3
  15.6 1.1 copy.47
  16.9 5.6 collective-permute-start.1
  22.5 1.1 bitcast_dynamic-update-slice_fusion
  23.6 0.7 convert_element_type.5
  24.4 0.7 broadcast_add_fusion
  25.4 206.0 %while.52 = (s32[]{:T(128)}, f32[8,16,512]{2,1,0:T(8,128)S(1)}, s32[8]{0:T(128)S(1)}, f32[16,6144]{1,0:T(8,128)S(1)}, f32[3,6144]{1,0:T(4,128)S(1)}, /*index=5*/...) while((s32[]{:T(128)}, f32[8,16,512]{2,1,0:T(8,128)S(1)}, ...), condition=%wide.region_1.2_spmd, body=%wide.region_0.1_spmd.sunk | while | flops 246620224 | bytes 1092197 | solution.py:58
  38.6 0.7 constant_dynamic-slice_fusion.141
  64.3 0.7 constant_dynamic-slice_fusion.141
  167.3 0.7 constant_dynamic-slice_fusion.141
  193.0 0.7 constant_dynamic-slice_fusion.141
  231.9 5.6 collective-permute-start.5
  237.9 1.8 collective-permute-done.4
  239.8 202.8 %while.53 = (s32[]{:T(128)}, f32[8,16,512]{2,1,0:T(8,128)S(1)}, s32[8]{0:T(128)S(1)}, f32[16,6144]{1,0:T(8,128)S(1)}, f32[3,6144]{1,0:T(4,128)S(1)}, /*index=5*/...) while((s32[]{:T(128)}, f32[8,16,512]{2,1,0:T(8,128)S(1)}, ...), condition=%wide.region_3.4_spmd, body=%wide.region_2.3_spmd.sunk | while | flops 246620224 | bytes 1092197 | solution.py:58
  442.8 6.1 collective-permute-start.7
  449.2 1.5 collective-permute-done.6
  450.9 203.8 %while.54 = (s32[]{:T(128)}, f32[8,16,512]{2,1,0:T(8,128)S(1)}, s32[8]{0:T(128)S(1)}, f32[16,6144]{1,0:T(8,128)S(1)}, f32[3,6144]{1,0:T(4,128)S(1)}, /*index=5*/...) while((s32[]{:T(128)}, f32[8,16,512]{2,1,0:T(8,128)S(1)}, ...), condition=%wide.region_5.6_spmd, body=%wide.region_4.5_spmd.sunk | while | flops 246620224 | bytes 1092197 | solution.py:58
  654.8 1.9 collective-permute-start.8
  656.7 4.4 collective-permute-start.9
  661.4 1.8 collective-permute-done.8
  663.4 207.7 %while.55 = (s32[]{:T(128)}, f32[8,16,512]{2,1,0:T(8,128)S(1)}, s32[8]{0:T(128)S(1)}, f32[16,6144]{1,0:T(8,128)S(1)}, f32[3,6144]{1,0:T(4,128)S(1)}, /*index=5*/...) while((s32[]{:T(128)}, f32[8,16,512]{2,1,0:T(8,128)S(1)}, ...), condition=%wide.region_7.8_spmd, body=%wide.region_6.7_spmd.sunk | while | flops 246620224 | bytes 1092197 | solution.py:58
  676.8 0.7 constant_dynamic-slice_fusion.159
  702.7 0.7 constant_dynamic-slice_fusion.159
  728.7 0.7 constant_dynamic-slice_fusion.159
  754.7 0.7 constant_dynamic-slice_fusion.159
  780.6 0.7 constant_dynamic-slice_fusion.159
  806.6 0.7 constant_dynamic-slice_fusion.159
  832.5 0.7 constant_dynamic-slice_fusion.159
  858.5 0.7 constant_dynamic-slice_fusion.159
  871.3 1.0 copy-done.4
  872.7 45.1 %all-gather.2.cloned.1.call-done = f32[5,32,4096]{2,1,0:T(8,128)} async-done(((f32[5,16,4096]{2,1,0:T(8,128)}), f32[5,32,4096]{2,1,0:T(8,128)}) %all-gather.2.cloned.1.call-update) | async-done | bytes 2621456 | tf_op jit(solution)/shard_map/all_gather | solution.py:117
  917.8 5.6 fusion.2577
  923.9 1.3 copy-done.1
  925.2 1.6 bitcast_add_fusion
  926.8 1122.0 %all-reduce.2.cloned.1.call-done = f32[160,160]{0,1:T(8,128)} async-done(((f32[160,160]{0,1:T(8,128)}), f32[160,160]{0,1:T(8,128)}) %all-reduce.2.cloned.1.call-update) | async-done | bytes 102416 | tf_op jit(solution)/shard_map/psum | solution.py:119
  2048.8 0.9 broadcast_multiply_fusion
  2049.9 11.7 cholesky.44
  2062.9 9.8 custom-call.10
  2074.0 12.0 cholesky.55
  2087.3 9.8 custom-call.11
  2097.8 2.7 fusion.2532
  2100.6 1.0 copy.29
  2101.6 1.1 convolution_bitcast_fusion.1
  2102.7 1.2 convolution_bitcast_fusion
  2103.9 2.0 copy.30
  2105.9 1.0 copy.28
  (936 shorter events, 413.4 us)
Async XLA Ops:
  7.2 910.6 %all-gather.2.cloned.1.call-start = ((), (), s32[]{:S(2)}) async-start(), calls=%async_computation | async-start | bytes 3932160 | tf_op jit(solution)/shard_map/all_gather | solution.py:117
  8.1 17.2 collective-permute-start.2
  10.3 15.0 collective-permute-start.3
  16.8 8.5 collective-permute-start
  16.9 8.4 collective-permute-start.1
  25.4 206.0 %copy-start.3 = (f32[16,1,4096]{2,1,0:T(1,128)S(1)}, f32[16,1,4096]{2,1,0:T(1,128)}, u32[]{:S(2)}) copy-start(f32[16,1,4096]{2,1,0:T(1,128)} %param.13) | copy-start | bytes 786436
  231.6 8.2 collective-permute-start.4
  231.9 7.9 collective-permute-start.5
  442.7 8.0 collective-permute-start.6
  442.8 8.0 collective-permute-start.7
  654.8 8.4 collective-permute-start.8
  656.7 6.6 collective-permute-start.9
  871.3 1.1 copy-start.4
  872.4 1176.4 %all-reduce.2.cloned.1.call-start = ((), (), s32[]{:S(2)}) async-start(), calls=%async_computation.1 | async-start | bytes 327680 | tf_op jit(solution)/shard_map/psum | solution.py:119
  917.8 5.6 copy-start
  923.9 1.3 copy-start.1
  2073.9 27.7 %copy-start.2 = (f32[4,32,4096]{2,1,0:T(8,128)S(1)}, f32[4,32,4096]{2,1,0:T(8,128)}, u32[]{:S(2)}) copy-start(f32[4,32,4096]{2,1,0:T(8,128)} %copy-done.1) | copy-start | bytes 6291460
Sparse Core Ops, SparseCore 0:
  872.5 45.1 all-gather.1
  923.5 1125.2 all-reduce.1
where the time goes:
time: 2130 us; the launch traced here: 2110 us
  waiting for transfers between devices  1170 us (55%)
  loops' own time  407 us (19%)
  matrix products  296 us (14%)
  local copies, waits for them, and re-layouts  140 us (7%)
  other arithmetic  51.7 us (2%)
  starting transfers between devices  32 us (2%)
    psum x1, waiting for transfers between devices, local(): gram = lax.psum(row_products(flat), ('blk', 'leaf'))  1120 us
    another operation x4, loops' own time, band_product(): lax.scan(turn, jnp.zeros((), jnp.int32), jnp.arange(8, dtype=jnp.int32))  407 us
    dot_general x576, matrix products, turn(): total = total + jnp.dot(near_field, tile, precision=exact)  284 us
    dynamic_slice x160, local copies, waits for them, and re-layouts, turn(): listed = lax.dynamic_index_in_dim(weights[offset], block, 0, False)  105 us
    all_gather x1, waiting for transfers between devices, local(): whole = lax.all_gather(half_panel, 'rhs', axis=1, tiled=True)  45.1 us
  transfers between devices with their start and end apart: 12, of which 7 were waited for; matrix products, arithmetic and copies ran while one was open for 0% of the time, Pallas kernels for 0%

commit v1 on v0

--- a/solution.py
+++ b/solution.py
@@ -116,7 +116,7 @@
     sides_here = field.shape[0]
     whole = lax.all_gather(half_panel, "rhs", axis=1, tiled=True)
     flat = whole.reshape(-1, own_rows)
-    gram = lax.psum(row_products(flat), ("blk", "leaf"))
+    gram = lax.psum(lax.psum(row_products(flat), "blk"), "leaf")
     inverse_low, combo = galerkin(gram, count_points, M)
     first_rows = flat[: S * M]
     image = flat[M:] + centre_shift * first_rows

time: 2130 us -> 1230 us (0.58)
  waiting for transfers between devices: 1170 us -> 263 us
    psum x1 -> x2, waiting for transfers between devices: 1120 us -> 213 us  [local(): gram = lax.psum(lax.psum(row_products(flat), 'blk'), 'leaf')]
  transfers between devices with their start and end apart: 12 -> 13, of which waited for: 7 -> 8; matrix products, arithmetic and copies ran while one was open for 0% -> 1% of each run, Pallas kernels for 0% -> 0%
where the time goes in v1:
time: 1230 us; the launch traced here: 1210 us
  loops' own time  411 us (33%)
  matrix products  296 us (24%)
  waiting for transfers between devices  263 us (21%)
  local copies, waits for them, and re-layouts  142 us (12%)
  other arithmetic  53.9 us (4%)
  starting transfers between devices  32.1 us (3%)
  between operations  14.7 us (1%)
    another operation x4, loops' own time, band_product(): lax.scan(turn, jnp.zeros((), jnp.int32), jnp.arange(8, dtype=jnp.int32))  411 us
    dot_general x576, matrix products, turn(): total = total + jnp.dot(near_field, tile, precision=exact)  284 us
    psum x2, waiting for transfers between devices, local(): gram = lax.psum(lax.psum(row_products(flat), 'blk'), 'leaf')  213 us
    dynamic_slice x160, local copies, waits for them, and re-layouts, turn(): listed = lax.dynamic_index_in_dim(weights[offset], block, 0, False)  105 us
    all_gather x1, waiting for transfers between devices, local(): whole = lax.all_gather(half_panel, 'rhs', axis=1, tiled=True)  45.3 us
    ppermute x5, starting transfers between devices, extended(): after = lax.ppermute(leading, axis, down)  27.2 us
  transfers between devices with their start and end apart: 13, of which 8 were waited for; matrix products, arithmetic and copies ran while one was open for 1% of the time, Pallas kernels for 0%

profile of v1, /device:TPU:2, one launch (start us, length us, event | category | flops | bytes accessed | tf_op | source)
XLA Modules:
  0.0 1213.0 jit_solution(9819237676339002979)
XLA Ops:
  7.2 0.8 copy.48
  8.1 2.2 collective-permute-start.2
  10.3 5.4 collective-permute-start.3
  15.6 1.1 copy.47
  16.9 5.6 collective-permute-start.1
  22.5 1.1 bitcast_dynamic-update-slice_fusion
  23.6 0.7 convert_element_type.5
  24.4 0.7 broadcast_add_fusion
  25.4 204.8 %while.52 = (s32[]{:T(128)}, f32[8,16,512]{2,1,0:T(8,128)S(1)}, s32[8]{0:T(128)S(1)}, f32[16,6144]{1,0:T(8,128)S(1)}, f32[3,6144]{1,0:T(4,128)S(1)}, /*index=5*/...) while((s32[]{:T(128)}, f32[8,16,512]{2,1,0:T(8,128)S(1)}, ...), condition=%wide.region_1.2_spmd, body=%wide.region_0.1_spmd.sunk | while | flops 246620224 | bytes 1092197 | solution.py:58
  230.8 5.6 collective-permute-start.5
  236.8 1.8 collective-permute-done.4
  238.7 205.5 %while.53 = (s32[]{:T(128)}, f32[8,16,512]{2,1,0:T(8,128)S(1)}, s32[8]{0:T(128)S(1)}, f32[16,6144]{1,0:T(8,128)S(1)}, f32[3,6144]{1,0:T(4,128)S(1)}, /*index=5*/...) while((s32[]{:T(128)}, f32[8,16,512]{2,1,0:T(8,128)S(1)}, ...), condition=%wide.region_3.4_spmd, body=%wide.region_2.3_spmd.sunk | while | flops 246620224 | bytes 1092197 | solution.py:58
  277.8 0.7 constant_dynamic-slice_fusion.147
  329.2 0.7 constant_dynamic-slice_fusion.147
  406.2 0.7 constant_dynamic-slice_fusion.147
  444.4 6.1 collective-permute-start.7
  450.8 1.5 collective-permute-done.6
  452.5 208.4 %while.54 = (s32[]{:T(128)}, f32[8,16,512]{2,1,0:T(8,128)S(1)}, s32[8]{0:T(128)S(1)}, f32[16,6144]{1,0:T(8,128)S(1)}, f32[3,6144]{1,0:T(4,128)S(1)}, /*index=5*/...) while((s32[]{:T(128)}, f32[8,16,512]{2,1,0:T(8,128)S(1)}, ...), condition=%wide.region_5.6_spmd, body=%wide.region_4.5_spmd.sunk | while | flops 246620224 | bytes 1092197 | solution.py:58
  466.0 0.7 constant_dynamic-slice_fusion.153
  492.1 0.7 constant_dynamic-slice_fusion.153
  518.1 0.7 constant_dynamic-slice_fusion.153
  544.2 0.7 constant_dynamic-slice_fusion.153
  570.2 0.7 constant_dynamic-slice_fusion.153
  596.3 0.7 constant_dynamic-slice_fusion.153
  622.3 0.7 constant_dynamic-slice_fusion.153
  648.4 0.7 constant_dynamic-slice_fusion.153
  661.0 1.9 collective-permute-start.8
  662.9 4.4 collective-permute-start.9
  667.6 1.8 collective-permute-done.8
  669.6 206.8 %while.55 = (s32[]{:T(128)}, f32[8,16,512]{2,1,0:T(8,128)S(1)}, s32[8]{0:T(128)S(1)}, f32[16,6144]{1,0:T(8,128)S(1)}, f32[3,6144]{1,0:T(4,128)S(1)}, /*index=5*/...) while((s32[]{:T(128)}, f32[8,16,512]{2,1,0:T(8,128)S(1)}, ...), condition=%wide.region_7.8_spmd, body=%wide.region_6.7_spmd.sunk | while | flops 246620224 | bytes 1092197 | solution.py:58
  876.7 1.1 copy-done.3
  877.8 45.3 %all-gather.2.cloned.1.call-done = f32[5,32,4096]{2,1,0:T(8,128)} async-done(((f32[5,16,4096]{2,1,0:T(8,128)}), f32[5,32,4096]{2,1,0:T(8,128)}) %all-gather.2.cloned.1.call-update) | async-done | bytes 2621456 | tf_op jit(solution)/shard_map/all_gather | solution.py:117
  923.1 5.6 fusion.2577
  929.0 2.6 fusion.2570
  931.6 154.6 %all-reduce.3.cloned.1.call-done = f32[160,160]{0,1:T(8,128)} async-done(((f32[160,160]{0,1:T(8,128)}), f32[160,160]{0,1:T(8,128)}) %all-reduce.3.cloned.1.call-update) | async-done | bytes 102416 | tf_op jit(solution)/shard_map/psum | solution.py:119
  1086.3 3.9 bitcast_add_fusion
  1090.1 57.9 %all-reduce.5.cloned.1.call-done = f32[160,160]{0,1:T(8,128)} async-done(((f32[160,160]{0,1:T(8,128)}), f32[160,160]{0,1:T(8,128)}) %all-reduce.5.cloned.1.call-update) | async-done | bytes 102416 | tf_op jit(solution)/shard_map/psum | solution.py:119
  1148.0 0.9 broadcast_multiply_fusion
  1149.1 11.7 cholesky.44
  1162.1 9.8 custom-call.10
  1173.2 11.7 cholesky.55
  1186.2 10.0 custom-call.11
  1197.0 2.7 fusion.2532
  1199.7 1.0 copy.29
  1200.7 1.1 convolution_bitcast_fusion.1
  1201.8 1.2 convolution_bitcast_fusion
  1203.0 2.0 copy.30
  1205.1 1.0 copy.28
  (937 shorter events, 414.9 us)
Async XLA Ops:
  7.2 916.0 %all-gather.2.cloned.1.call-start = ((), (), s32[]{:S(2)}) async-start(), calls=%async_computation | async-start | bytes 3932160 | tf_op jit(solution)/shard_map/all_gather | solution.py:117
  8.1 17.2 %collective-permute-start.2 = (f32[3,1024]{1,0:T(4,128)S(1)}, f32[3,1024]{1,0:T(4,128)S(1)}, u32[]{:S(2)}, u32[]{:S(2)}) collective-permute-start(f32[3,1024]{1,0:T(4,128)S(1)} %get-tuple-element.898), channel_id=1, source_target_pairs={{0,16},{16,32},{32,48},{48,64},{64,80},{80,96},{96,112},{112,128},... | collective-permute-start | bytes 36872 | tf_op jit(solution)/shard_map/ppermute | solution.py:23
  10.3 15.0 %collective-permute-start.3 = (f32[3,1024]{1,0:T(4,128)S(1)}, f32[3,1024]{1,0:T(4,128)S(1)}, u32[]{:S(2)}, u32[]{:S(2)}) collective-permute-start(f32[3,1024]{1,0:T(4,128)S(1)} %get-tuple-element.899), channel_id=1, source_target_pairs={{16,0},{32,16},{48,32},{64,48},{80,64},{96,80},{112,96},{128,112},... | collective-permute-start | bytes 36872 | tf_op jit(solution)/shard_map/ppermute | solution.py:24
  16.8 8.5 collective-permute-start
  16.9 8.4 collective-permute-start.1
  25.4 204.9 %copy-start.2 = (f32[16,1,4096]{2,1,0:T(1,128)S(1)}, f32[16,1,4096]{2,1,0:T(1,128)}, u32[]{:S(2)}) copy-start(f32[16,1,4096]{2,1,0:T(1,128)} %param.13) | copy-start | bytes 786436
  230.5 8.2 collective-permute-start.4
  230.8 7.9 collective-permute-start.5
  444.3 8.0 collective-permute-start.6
  444.4 8.0 collective-permute-start.7
  661.0 8.4 collective-permute-start.8
  662.9 6.6 collective-permute-start.9
  876.7 1.1 copy-start.3
  877.8 208.5 %all-reduce.3.cloned.1.call-start = ((), (), s32[]{:S(2)}) async-start(), calls=%async_computation.1 | async-start | bytes 327680 | tf_op jit(solution)/shard_map/psum | solution.py:119
  923.1 5.9 copy-start
  928.8 219.2 %all-reduce.5.cloned.1.call-start = ((), (), s32[]{:S(2)}) async-start(), calls=%async_computation.2 | async-start | bytes 327680 | tf_op jit(solution)/shard_map/psum | solution.py:119
  1173.1 27.7 %copy-start.1 = (f32[4,32,4096]{2,1,0:T(8,128)S(1)}, f32[4,32,4096]{2,1,0:T(8,128)}, u32[]{:S(2)}) copy-start(f32[4,32,4096]{2,1,0:T(8,128)} %get-tuple-element.889) | copy-start | bytes 6291460
Sparse Core Ops, SparseCore 0:
  877.9 45.1 all-gather.1
  928.9 157.3 all-reduce.2
  1088.7 59.2 all-reduce.4
